TPU v7x, 32 devices: a whole 2x2x4 slice. The times are simulated.
32 devices in a mesh: group: 2 (over x), src: 8 (over z, y), tile: 2 (over core).
Axes of the slice: x: 2, y: 2, z: 4, core: 2. Of those that a mesh axis runs over, the one named last changes fastest.
Arguments:
- near_field: bfloat16 [4, 64, 2, 3, 512], P(('group', 'tile'), 'src'), parts along dimension 0, may hold values from -6 to 6
- x_taps: bfloat16 [8, 2, 8, 65], P('src'), may hold values from -0.5 to 0.5
- y_taps: bfloat16 [8, 2, 8, 65], P('src'), may hold values from -0.1875 to 0.1875
- source_weight: float32 [8], P('src'), may hold values from 0.0125 to 0.125
Outputs:
- intensity: float32 [4, 64, 512], P(('group', 'tile'), 'src'), parts along dimension 0
There are 2 independent parts, one for each index of `group`. A program takes and returns all parts, laid end to end along the dimension named above; an argument that names none is the same for every part. Nothing has to cross between parts.
All inputs are finite; a program needn't handle non-finite values.
Results may differ from a plain program's by a relative error of at most 0.00054.
Values may be sent and summed in bfloat16 or wider, within the bound.
A program may use at most 128 MiB of HBM per device.

v0:
```python
import jax
import jax.numpy as jnp
from jax import lax
from jax.sharding import PartitionSpec as P


def padded_2(cells, sides, width):
    for axis, dim in sides:
        count = lax.axis_size(axis)
        ends = count - 1
        head = lax.slice_in_dim(cells, 0, width, axis=dim)
        tail = lax.slice_in_dim(cells, cells.shape[dim] - width, cells.shape[dim], axis=dim)
        cells = jnp.concatenate(
            [
                lax.ppermute(tail, axis, [(i, (i + 1) % count) for i in range(ends)]),
                cells,
                lax.ppermute(head, axis, [((i + 1) % count, i) for i in range(ends)]),
            ],
            axis=dim,
        )
    return cells


def column_mats(taps):
    tap_count = taps.shape[-1]
    shift = lax.broadcasted_iota(jnp.int32, (tap_count, 256, 128), 0)
    inner = lax.broadcasted_iota(jnp.int32, (tap_count, 256, 128), 1)
    outer = lax.broadcasted_iota(jnp.int32, (tap_count, 256, 128), 2)
    select = (inner - outer == shift).astype(jnp.float32)
    coef = jnp.einsum(
        "xprt,tqj->xpqrj", taps.astype(jnp.float32), select, precision=lax.Precision.HIGHEST
    )
    real_part, imag_part = (coef[:, 0], coef[:, 1])
    full = jnp.stack(
        [jnp.stack([real_part, imag_part], axis=2), jnp.stack([-imag_part, real_part], axis=2)],
        axis=1,
    ).astype(jnp.bfloat16)
    return (full[:, :, :128], full[:, :, 128:])


def column_pass(rows_field, lower_mat, upper_mat, rim_width):
    count_rows, _, comps, width = rows_field.shape
    padded = jnp.pad(rows_field, ((0, 0), (0, 0), (0, 0), (rim_width, 128 - rim_width)))
    pieces = padded.reshape(count_rows, 2, comps, width // 128 + 1, 128)
    result = jnp.einsum(
        "ipcbq,xpqsrj->ixsrcbj", pieces[:, :, :, :-1], lower_mat, preferred_element_type=jnp.float32
    )
    result = result + jnp.einsum(
        "ipcbq,xpqsrj->ixsrcbj", pieces[:, :, :, 1:], upper_mat, preferred_element_type=jnp.float32
    )
    sources, ranks = (lower_mat.shape[0], lower_mat.shape[4])
    return result.reshape(count_rows, sources, 2, ranks, comps, width).astype(jnp.bfloat16)


def row_matrices(taps, block_rows, rim_width):
    tap_count = taps.shape[-1]
    span = block_rows + 2 * rim_width
    shift = lax.broadcasted_iota(jnp.int32, (tap_count, block_rows, span), 0)
    out_row = lax.broadcasted_iota(jnp.int32, (tap_count, block_rows, span), 1)
    in_row = lax.broadcasted_iota(jnp.int32, (tap_count, block_rows, span), 2)
    select = (in_row - out_row == shift).astype(jnp.float32)
    coef = jnp.einsum(
        "xprt,tik->xpirk", taps.astype(jnp.float32), select, precision=lax.Precision.HIGHEST
    )
    real_part, imag_part = (coef[:, 0], coef[:, 1])
    full = jnp.stack(
        [jnp.stack([real_part, -imag_part], axis=2), jnp.stack([imag_part, real_part], axis=2)],
        axis=1,
    )
    return full.astype(jnp.bfloat16)


def per_device(near_field, x_taps, y_taps, source_weight):
    rim_width = (x_taps.shape[-1] - 1) // 2
    width = near_field.shape[-1]
    local_rows = near_field.shape[1]
    whole_tile = lax.all_gather(near_field, "src", axis=1, tiled=True)
    padded_field = padded_2(whole_tile, (("tile", 1),), rim_width)
    lower_mat, upper_mat = column_mats(x_taps)
    padded_pass = column_pass(padded_field[0], lower_mat, upper_mat, rim_width)
    tile_rows = padded_pass.shape[0] - 2 * rim_width
    block_rows = 64
    row_mats = row_matrices(y_taps, block_rows, rim_width)

    def one_block(index):
        first_row = index * block_rows
        window = lax.dynamic_slice_in_dim(padded_pass, first_row, block_rows + 2 * rim_width, 0)
        image = jnp.einsum(
            "xoiprk,kxprcw->xoicw", row_mats, window, preferred_element_type=jnp.float32
        )
        power = jnp.sum(image * image, axis=(1, 3))
        return jnp.sum(source_weight[:, None, None] * power, axis=0)

    blocks = lax.map(one_block, jnp.arange(tile_rows // block_rows, dtype=jnp.int32))
    own_image = blocks.reshape(tile_rows, width)
    summed = lax.psum_scatter(own_image, "src", scatter_dimension=0, tiled=True)
    return summed.reshape(1, local_rows, width)


def solution(mesh):
    placed = (
        P(("group", "tile"), "src", None, None, None),
        P("src", None, None, None),
        P("src", None, None, None),
        P("src"),
    )
    return jax.shard_map(
        per_device,
        mesh=mesh,
        in_specs=placed,
        out_specs=P(("group", "tile"), "src", None),
        check_vma=False,
    )
```

profile of v0, /device:TPU:0, one launch (start us, length us, event | category | flops | bytes accessed | tf_op | source)
XLA Modules:
  0.0 142.8 jit_solution(395169081686979123)
XLA Ops:
  6.5 0.0 copy-start
  6.5 0.0 reduce-scatter.2.cloned.1.call-start
  6.5 33.1 %all_gather.3 = bf16[1,64,2,3,512]{4,2,3,0,1:T(2,128)(2,1)S(1)} all-gather(bf16[1,8,2,3,512]{4,2,3,0,1:T(2,128)(2,1)} %bitcast.120), channel_id=1, replica_groups=mesh['group'=2,'src'=8,'tile'=2] {'src'}, dimensions={1}, use_global_device_ids=true | all-gather | bytes 442368 | tf_op jit(solution)/shard_map/all_gather | solution.py:77
  39.6 0.3 fusion.45
  39.9 0.7 copy.29
  40.6 2.0 %collective-permute-start = (bf16[1,32,2,3,512]{4,1,3,2,0:T(8,128)(2,1)}, bf16[1,32,2,3,512]{4,1,3,2,0:T(8,128)(2,1)}, u32[]{:S(2)}, u32[]{:S(2)}) collective-permute-start(bf16[1,32,2,3,512]{4,1,3,2,0:T(8,128)(2,1)} %copy.29), channel_id=1, source_target_pairs={{0,1},{2,3},{4,5},{6,7},{8,9},{10,11},{12,13},{14,15},{16,17},{18,... | collective-permute-start | bytes 589832 | tf_op jit(solution)/shard_map/ppermute | solution.py:15
  42.6 0.7 copy.30
  43.3 1.3 collective-permute-start.1
  44.6 0.0 copy-done
  44.6 1.1 fusion.9
  45.7 0.0 copy-start.2
  45.7 0.1 fusion.36
  45.9 0.1 fusion.35
  45.9 0.5 copy-done.2
  46.4 0.5 fusion.18
  47.0 1.1 maximum_bitcast_fusion.1
  48.1 0.8 maximum_bitcast_fusion.3
  49.0 1.3 copy.32
  50.9 1.4 fusion.26
  52.3 0.0 copy-start.1
  52.3 0.0 collective-permute-done
  52.3 2.2 %copy.31 = bf16[1,32,2,3,512]{1,4,3,2,0:T(8,128)(2,1)} copy(bf16[1,32,2,3,512]{4,1,3,2,0:T(8,128)(2,1)} %collective-permute-done) | data formatting | bytes 393216 | tf_op jit(solution)/shard_map/ppermute | solution.py:15
  54.5 0.0 collective-permute-done.1
  54.5 2.1 %copy.33 = bf16[1,32,2,3,512]{1,4,3,2,0:T(8,128)(2,1)} copy(bf16[1,32,2,3,512]{4,1,3,2,0:T(8,128)(2,1)} %collective-permute-done.1) | data formatting | bytes 393216 | tf_op jit(solution)/shard_map/ppermute | solution.py:17
  56.6 0.0 copy-done.1
  56.6 2.1 %maximum_bitcast_fusion.2 = bf16[128,2,3,512]{0,3,2,1:T(8,128)(2,1)S(1)} fusion(bf16[1,32,2,3,512]{1,4,3,2,0:T(8,128)(2,1)} %copy.33, bf16[1,64,2,3,512]{1,4,3,2,0:T(8,128)(2,1)S(1)} %copy-done.1, bf16[1,32,2,3,512]{1,4,3,2,0:T(8,128)(2,1)} %copy.31), kind=kLoop, calls=%fused_computation.31 | loop fusion | flops 2359296 | bytes 1572864 | tf_op jit(solution)/shard_map/squeeze | solution.py:80
  58.7 0.1 pad.4
  58.8 1.1 fusion.44
  59.9 1.2 copy.61
  61.1 1.5 %copy.62 = bf16[128,2,3,4,128]{4,0,1,3,2:T(8,128)(2,1)S(1)} copy(bf16[128,2,3,4,128]{0,4,3,2,1:T(8,128)(2,1)} %get-tuple-element.24) | data formatting | bytes 1572864
  62.6 3.0 %fusion.29 = f32[2,8,128,128,3,4,1]{3,2,6,5,4,1,0:T(8,128)S(1)} fusion(bf16[2,128,2,8,128,1,1]{4,3,1,2,0,6,5:T(8,128)(2,1)S(1)} %get-tuple-element.14, bf16[128,2,3,4,128]{4,0,1,3,2:T(8,128)(2,1)} %copy.61), kind=kOutput, calls=%fused_computation.26 | convolution fusion | flops 1610612736 | bytes 14417920 | tf_op jit(solution)/shard_map/ipcbq,xpqsrj->ixsrcbj/dot_general | solution.py:45
  65.6 2.3 %fusion = bf16[2,8,128,128,3,4]{3,2,5,4,1,0:T(8,128)(2,1)S(1)} fusion(f32[2,8,128,128,3,4,1]{3,2,6,5,4,1,0:T(8,128)S(1)} %fusion.29, bf16[2,128,2,8,128,1,1]{4,3,1,2,0,6,5:T(8,128)(2,1)S(1)} %get-tuple-element.13, bf16[128,2,3,4,128]{4,0,1,3,2:T(8,128)(2,1)S(1)} %copy.62), kind=kOutput, calls=%fused_computation.1 | convolution fusion | flops 1616904192 | bytes 20709376 | tf_op jit(solution)/shard_map/ipcbq,xpqsrj->ixsrcbj/dot_general | solution.py:48
  67.9 3.2 %fusion.21 = f32[64,512]{1,0:T(8,128)S(1)} fusion(bf16[128,2,8,3,512,1]{0,4,3,2,1,5:T(8,128)(2,1)S(1)} %bitcast.119, bf16[2,64,2,8,128,1]{4,3,1,2,0,5:T(8,128)(2,1)} %maximum_bitcast_fusion.3), kind=kOutput, calls=%fused_computation.16 | convolution fusion | flops 805666816 | bytes 6946816 | tf_op jit(solution)/shard_map/while/body/eval_jaxpr/xoiprk,kxprcw->xoicw/dot_general | solution.py:88
  71.1 0.7 broadcast_multiply_fusion
  71.8 0.0 reduce-scatter.2.cloned.1.call-update
  71.8 64.1 %reduce-scatter.2.cloned.1.call-done = f32[8,512]{1,0:T(8,128)} async-done(((f32[64,512]{1,0:T(8,128)}), f32[8,512]{1,0:T(8,128)}) %reduce-scatter.2.cloned.1.call-update) | async-done | bytes 16400 | tf_op jit(solution)/shard_map/reduce_scatter | solution.py:96
  (2 shorter events, 0.1 us)
Async XLA Ops:
  6.5 38.0 %copy-start = (bf16[1,2,8,65]{3,2,1,0:T(8,128)(2,1)S(1)}, bf16[1,2,8,65]{3,2,1,0:T(8,128)(2,1)}, u32[]{:S(2)}) copy-start(bf16[1,2,8,65]{3,2,1,0:T(8,128)(2,1)} %param.5) | copy-start | bytes 6244
  6.5 129.4 %reduce-scatter.2.cloned.1.call-start = ((), (), s32[]{:S(2)}) async-start(), calls=%async_computation.1 | async-start | bytes 147456 | tf_op jit(solution)/shard_map/reduce_scatter | solution.py:96
  40.6 11.8 %collective-permute-start = (bf16[1,32,2,3,512]{4,1,3,2,0:T(8,128)(2,1)}, bf16[1,32,2,3,512]{4,1,3,2,0:T(8,128)(2,1)}, u32[]{:S(2)}, u32[]{:S(2)}) collective-permute-start(bf16[1,32,2,3,512]{4,1,3,2,0:T(8,128)(2,1)} %copy.29), channel_id=1, source_target_pairs={{0,1},{2,3},{4,5},{6,7},{8,9},{10,11},{12,13},{14,15},{16,17},{18,... | collective-permute-start | bytes 589832 | tf_op jit(solution)/shard_map/ppermute | solution.py:15
  43.3 11.2 %collective-permute-start.1 = (bf16[1,32,2,3,512]{4,1,3,2,0:T(8,128)(2,1)}, bf16[1,32,2,3,512]{4,1,3,2,0:T(8,128)(2,1)}, u32[]{:S(2)}, u32[]{:S(2)}) collective-permute-start(bf16[1,32,2,3,512]{4,1,3,2,0:T(8,128)(2,1)} %copy.30), channel_id=1, source_target_pairs={{1,0},{3,2},{5,4},{7,6},{9,8},{11,10},{13,12},{15,14},{17,16},{19,... | collective-permute-start | bytes 589832 | tf_op jit(solution)/shard_map/ppermute | solution.py:17
  45.7 0.7 copy-start.2
  52.3 4.3 %copy-start.1 = (bf16[1,64,2,3,512]{1,4,3,2,0:T(8,128)(2,1)S(1)}, bf16[1,64,2,3,512]{1,4,3,2,0:T(8,128)(2,1)}, u32[]{:S(2)}) copy-start(bf16[1,64,2,3,512]{1,4,3,2,0:T(8,128)(2,1)} %copy.32) | copy-start | bytes 1179652
Sparse Core Ops, SparseCore 0:
  71.9 63.9 reduce-scatter.1
where the time goes:
time: 143 us
  waiting for transfers between devices  64.1 us (45%)
  blocking collectives  33.1 us (23%)
  between operations  14.2 us (10%)
  local copies, waits for them, and re-layouts  11.8 us (8%)
  matrix products  10.1 us (7%)
  other arithmetic  6.23 us (4%)
  starting transfers between devices  3.26 us (2%)
    reduce_scatter x1, waiting for transfers between devices, per_device(): summed = lax.psum_scatter(own_image, 'src', scatter_dimension=0, tiled=True)  64.1 us
    all_gather x1, blocking collectives, per_device(): whole_tile = lax.all_gather(near_field, 'src', axis=1, tiled=True)  33.1 us
    dot_general x1, matrix products, one_block(): jnp.einsum('xoiprk,kxprcw->xoicw', row_mats, window, preferred_element_ty...  3.22 us
    unnamed x8, local copies, waits for them, and re-layouts  3.17 us
    dot_general x1, matrix products, column_pass(): jnp.einsum('ipcbq,xpqsrj->ixsrcbj', pieces[:, :, :, :-1], lower_mat, pref...  2.99 us
  transfers between devices with their start and end apart: 3, of which 1 were waited for; matrix products, arithmetic and copies ran while one was open for 7% of the time, Pallas kernels for 0%

commit v1 on v0

--- a/solution.py
+++ b/solution.py
@@ -74,7 +74,26 @@
     rim_width = (x_taps.shape[-1] - 1) // 2
     width = near_field.shape[-1]
     local_rows = near_field.shape[1]
-    whole_tile = lax.all_gather(near_field, "src", axis=1, tiled=True)
+    size, place, width_2 = (lax.axis_size("src"), lax.axis_index("src"), near_field.shape[1])
+    forward = [(i_2, (i_2 + 1) % size) for i_2 in range(size)]
+    left = [(i_2, (i_2 - 1) % size) for i_2 in range(size)]
+    whole = jnp.zeros(
+        (*near_field.shape[:1], size * width_2, *near_field.shape[1 + 1 :]), near_field.dtype
+    )
+    whole = lax.dynamic_update_slice_in_dim(whole, near_field, place * width_2, axis=1)
+    from_left = from_right = near_field
+    half = size // 2
+    for step in range(1, half + 1):
+        from_left = lax.ppermute(from_left, "src", forward)
+        whole = lax.dynamic_update_slice_in_dim(
+            whole, from_left, (place - step) % size * width_2, axis=1
+        )
+        if step < size - half:
+            from_right = lax.ppermute(from_right, "src", left)
+            whole = lax.dynamic_update_slice_in_dim(
+                whole, from_right, (place + step) % size * width_2, axis=1
+            )
+    whole_tile = whole
     padded_field = padded_2(whole_tile, (("tile", 1),), rim_width)
     lower_mat, upper_mat = column_mats(x_taps)
     padded_pass = column_pass(padded_field[0], lower_mat, upper_mat, rim_width)

time: 143 us -> 172 us (1.20)
  local copies, waits for them, and re-layouts: 11.8 us -> 54 us
  blocking collectives: 33.1 us -> 0 us
  starting transfers between devices: 3.26 us -> 19.3 us
  waiting for transfers between devices: 64.1 us -> 67.5 us
    dynamic_update_slice x0 -> x8, local copies, waits for them, and re-layouts: none -> 37.7 us  [the longest x4 20.1 us: per_device(): lax.dynamic_update_slice_in_dim(whole, from_left, (place - step) % size *...]
    all_gather x1 -> x0, blocking collectives: 33.1 us -> none  [per_device(): whole_tile = lax.all_gather(near_field, 'src', axis=1, tiled=True)]
    ppermute x0 -> x7, starting transfers between devices: none -> 15.9 us  [the longest x3 12.8 us: per_device(): from_right = lax.ppermute(from_right, 'src', left)]
    ppermute x0 -> x7, waiting for transfers between devices: none -> 3.06 us  [the longest x4 2.66 us: per_device(): from_left = lax.ppermute(from_left, 'src', forward)]
    ppermute x0 -> x7, local copies, waits for them, and re-layouts: none -> 2.59 us  [the longest x4 1.48 us: per_device(): from_left = lax.ppermute(from_left, 'src', forward)]
    unnamed x8 -> x12, local copies, waits for them, and re-layouts: 3.17 us -> 5.52 us
  transfers between devices with their start and end apart: 3 -> 10, of which waited for: 1 -> 4; matrix products, arithmetic and copies ran while one was open for 7% -> 26% of each run, Pallas kernels for 0% -> 0%
where the time goes in v1:
time: 172 us
  waiting for transfers between devices  67.5 us (39%)
  local copies, waits for them, and re-layouts  54 us (31%)
  starting transfers between devices  19.3 us (11%)
  between operations  14.4 us (8%)
  matrix products  9 us (5%)
  other arithmetic  7.28 us (4%)
    reduce_scatter x1, waiting for transfers between devices, per_device(): summed = lax.psum_scatter(own_image, 'src', scatter_dimension=0, tiled=True)  64.4 us
    dynamic_update_slice x4, local copies, waits for them, and re-layouts, per_device(): lax.dynamic_update_slice_in_dim(whole, from_left, (place - step) % size *...  20.1 us
    dynamic_update_slice x3, local copies, waits for them, and re-layouts, per_device(): lax.dynamic_update_slice_in_dim(whole, from_right, (place + step) % size...  15.1 us
    ppermute x3, starting transfers between devices, per_device(): from_right = lax.ppermute(from_right, 'src', left)  12.8 us
    unnamed x12, local copies, waits for them, and re-layouts  5.52 us
  transfers between devices with their start and end apart: 10, of which 4 were waited for; matrix products, arithmetic and copies ran while one was open for 26% of the time, Pallas kernels for 0%

profile of v1, /device:TPU:0, one launch (start us, length us, event | category | flops | bytes accessed | tf_op | source)
XLA Modules:
  0.0 171.5 jit_solution(4542771930146322577)
XLA Ops:
  6.5 0.8 copy.31
  7.4 3.0 %collective-permute-start = (bf16[1,8,2,3,512]{4,1,3,2,0:T(8,128)(2,1)S(1)}, bf16[1,8,2,3,512]{4,1,3,2,0:T(8,128)(2,1)S(1)}, u32[]{:S(2)}, u32[]{:S(2)}) collective-permute-start(bf16[1,8,2,3,512]{4,1,3,2,0:T(8,128)(2,1)S(1)} %copy.31), channel_id=1, source_target_pairs={{0,2},{2,4},{4,6},{6,8},{8,10},{10,12},{12,14},{14,0},{1,3},{3,5},... | collective-permute-start | bytes 147464 | tf_op jit(solution)/shard_map/ppermute | solution.py:87
  10.3 3.1 %collective-permute-start.1 = (bf16[1,8,2,3,512]{4,1,3,2,0:T(8,128)(2,1)S(1)}, bf16[1,8,2,3,512]{4,1,3,2,0:T(8,128)(2,1)S(1)}, u32[]{:S(2)}, u32[]{:S(2)}) collective-permute-start(bf16[1,8,2,3,512]{4,1,3,2,0:T(8,128)(2,1)S(1)} %copy.31), channel_id=1, source_target_pairs={{0,14},{2,0},{4,2},{6,4},{8,6},{10,8},{12,10},{14,12},{1,15},{3,1}... | collective-permute-start | bytes 147464 | tf_op jit(solution)/shard_map/ppermute | solution.py:92
  13.4 1.1 fusion.9
  14.6 0.1 fusion.36
  14.8 0.5 copy-done.3
  15.3 0.5 fusion.18
  15.8 0.7 fusion.40
  16.6 4.7 %collective-permute-start.3 = (bf16[1,8,2,3,512]{4,1,3,2,0:T(8,128)(2,1)S(1)}, bf16[1,8,2,3,512]{4,1,3,2,0:T(8,128)(2,1)S(1)}, u32[]{:S(2)}, u32[]{:S(2)}) collective-permute-start(bf16[1,8,2,3,512]{4,1,3,2,0:T(8,128)(2,1)S(1)} %collective-permute-done.1), channel_id=1, source_target_pairs={{0,14},{2,0},{4,2},{6,4},{8,6},{10,8},{12,10},{14,12},{1,15},{3,1}... | collective-permute-start | bytes 147464 | tf_op jit(solution)/shard_map/ppermute | solution.py:92
  21.3 1.3 collective-permute-done.2
  22.6 0.4 collective-permute-done.3
  23.0 5.0 %collective-permute-start.5 = (bf16[1,8,2,3,512]{4,1,3,2,0:T(8,128)(2,1)S(1)}, bf16[1,8,2,3,512]{4,1,3,2,0:T(8,128)(2,1)S(1)}, u32[]{:S(2)}, u32[]{:S(2)}) collective-permute-start(bf16[1,8,2,3,512]{4,1,3,2,0:T(8,128)(2,1)S(1)} %collective-permute-done.3), channel_id=1, source_target_pairs={{0,14},{2,0},{4,2},{6,4},{8,6},{10,8},{12,10},{14,12},{1,15},{3,1}... | collective-permute-start | bytes 147464 | tf_op jit(solution)/shard_map/ppermute | solution.py:92
  28.1 1.3 collective-permute-done.4
  29.4 1.2 maximum_bitcast_fusion.1
  30.6 0.4 copy.30
  31.2 2.5 %dynamic_update_slice.27 = bf16[1,64,2,3,512]{1,4,3,2,0:T(8,128)(2,1)S(1)} dynamic-update-slice(bf16[1,64,2,3,512]{1,4,3,2,0:T(8,128)(2,1)S(1)} %broadcast_in_dim.9, bf16[1,8,2,3,512]{1,4,3,2,0:T(8,128)(2,1)S(1)} %copy.30, s32[]{:T(128)} %constant.67.clone.1, s32[]{:T(128)S(6)} %select_n.57, s32[]{:T(128)} %constant.67.clone.1, s32[]{:T(128)} %constant.67.clone.1, s32[]{:T(128)} %constant.67.clone.1) | dynamic-update-slice | bytes 98308 | tf_op jit(solution)/shard_map/dynamic_update_slice | solution.py:83
  33.7 0.4 copy.32
  34.1 5.0 %dynamic_update_slice.28 = bf16[1,64,2,3,512]{1,4,3,2,0:T(8,128)(2,1)S(1)} dynamic-update-slice(bf16[1,64,2,3,512]{1,4,3,2,0:T(8,128)(2,1)S(1)} %dynamic_update_slice.27, bf16[1,8,2,3,512]{1,4,3,2,0:T(8,128)(2,1)S(1)} %copy.32, s32[]{:T(128)} %constant.67.clone.1, s32[]{:T(128)S(6)} %select_n.59, s32[]{:T(128)} %constant.67.clone.1, s32[]{:T(128)} %constant.67.clone.1, s32[]{:T(128)} %constant.67.clone.1) | dynamic-update-slice | bytes 98308 | tf_op jit(solution)/shard_map/dynamic_update_slice | solution.py:88
  39.2 0.4 copy.34
  39.5 5.0 %dynamic_update_slice.29 = bf16[1,64,2,3,512]{1,4,3,2,0:T(8,128)(2,1)S(1)} dynamic-update-slice(bf16[1,64,2,3,512]{1,4,3,2,0:T(8,128)(2,1)S(1)} %dynamic_update_slice.28, bf16[1,8,2,3,512]{1,4,3,2,0:T(8,128)(2,1)S(1)} %copy.34, s32[]{:T(128)} %constant.67.clone.1, s32[]{:T(128)S(6)} %select_n.61, s32[]{:T(128)} %constant.67.clone.1, s32[]{:T(128)} %constant.67.clone.1, s32[]{:T(128)} %constant.67.clone.1) | dynamic-update-slice | bytes 98308 | tf_op jit(solution)/shard_map/dynamic_update_slice | solution.py:93
  44.6 0.4 copy.35
  44.9 5.0 %dynamic_update_slice.30 = bf16[1,64,2,3,512]{1,4,3,2,0:T(8,128)(2,1)S(1)} dynamic-update-slice(bf16[1,64,2,3,512]{1,4,3,2,0:T(8,128)(2,1)S(1)} %dynamic_update_slice.29, bf16[1,8,2,3,512]{1,4,3,2,0:T(8,128)(2,1)S(1)} %copy.35, s32[]{:T(128)} %constant.67.clone.1, s32[]{:T(128)S(6)} %select_n.63, s32[]{:T(128)} %constant.67.clone.1, s32[]{:T(128)} %constant.67.clone.1, s32[]{:T(128)} %constant.67.clone.1) | dynamic-update-slice | bytes 98308 | tf_op jit(solution)/shard_map/dynamic_update_slice | solution.py:88
  50.0 0.4 copy.36
  50.3 5.0 %dynamic_update_slice.31 = bf16[1,64,2,3,512]{1,4,3,2,0:T(8,128)(2,1)S(1)} dynamic-update-slice(bf16[1,64,2,3,512]{1,4,3,2,0:T(8,128)(2,1)S(1)} %dynamic_update_slice.30, bf16[1,8,2,3,512]{1,4,3,2,0:T(8,128)(2,1)S(1)} %copy.36, s32[]{:T(128)} %constant.67.clone.1, s32[]{:T(128)S(6)} %select_n.65, s32[]{:T(128)} %constant.67.clone.1, s32[]{:T(128)} %constant.67.clone.1, s32[]{:T(128)} %constant.67.clone.1) | dynamic-update-slice | bytes 98308 | tf_op jit(solution)/shard_map/dynamic_update_slice | solution.py:93
  55.4 0.4 copy.37
  55.8 5.0 %dynamic_update_slice.32 = bf16[1,64,2,3,512]{1,4,3,2,0:T(8,128)(2,1)S(1)} dynamic-update-slice(bf16[1,64,2,3,512]{1,4,3,2,0:T(8,128)(2,1)S(1)} %dynamic_update_slice.31, bf16[1,8,2,3,512]{1,4,3,2,0:T(8,128)(2,1)S(1)} %copy.37, s32[]{:T(128)} %constant.67.clone.1, s32[]{:T(128)S(6)} %select_n.67, s32[]{:T(128)} %constant.67.clone.1, s32[]{:T(128)} %constant.67.clone.1, s32[]{:T(128)} %constant.67.clone.1) | dynamic-update-slice | bytes 98308 | tf_op jit(solution)/shard_map/dynamic_update_slice | solution.py:88
  60.8 0.4 copy.38
  61.2 5.0 %dynamic_update_slice.33 = bf16[1,64,2,3,512]{1,4,3,2,0:T(8,128)(2,1)S(1)} dynamic-update-slice(bf16[1,64,2,3,512]{1,4,3,2,0:T(8,128)(2,1)S(1)} %dynamic_update_slice.32, bf16[1,8,2,3,512]{1,4,3,2,0:T(8,128)(2,1)S(1)} %copy.38, s32[]{:T(128)} %constant.67.clone.1, s32[]{:T(128)S(6)} %select_n.69, s32[]{:T(128)} %constant.67.clone.1, s32[]{:T(128)} %constant.67.clone.1, s32[]{:T(128)} %constant.67.clone.1) | dynamic-update-slice | bytes 98308 | tf_op jit(solution)/shard_map/dynamic_update_slice | solution.py:93
  66.2 0.4 copy.39
  66.6 5.0 %dynamic_update_slice.34 = bf16[1,64,2,3,512]{1,4,3,2,0:T(8,128)(2,1)S(1)} dynamic-update-slice(bf16[1,64,2,3,512]{1,4,3,2,0:T(8,128)(2,1)S(1)} %dynamic_update_slice.33, bf16[1,8,2,3,512]{1,4,3,2,0:T(8,128)(2,1)S(1)} %copy.39, s32[]{:T(128)} %constant.67.clone.1, s32[]{:T(128)S(6)} %select_n.71, s32[]{:T(128)} %constant.67.clone.1, s32[]{:T(128)} %constant.67.clone.1, s32[]{:T(128)} %constant.67.clone.1) | dynamic-update-slice | bytes 98308 | tf_op jit(solution)/shard_map/dynamic_update_slice | solution.py:88
  71.6 0.3 fusion.45
  71.9 0.9 copy.40
  72.9 2.0 %collective-permute-start.7 = (bf16[1,32,2,3,512]{4,1,3,2,0:T(8,128)(2,1)}, bf16[1,32,2,3,512]{4,1,3,2,0:T(8,128)(2,1)}, u32[]{:S(2)}, u32[]{:S(2)}) collective-permute-start(bf16[1,32,2,3,512]{4,1,3,2,0:T(8,128)(2,1)} %copy.40), channel_id=1, source_target_pairs={{0,1},{2,3},{4,5},{6,7},{8,9},{10,11},{12,13},{14,15},{16,17},{18,... | collective-permute-start | bytes 589832 | tf_op jit(solution)/shard_map/ppermute | solution.py:15
  74.9 0.9 copy.41
  75.8 1.5 collective-permute-start.8
  77.3 1.1 maximum_bitcast_fusion.3
  79.0 2.4 %fusion.26 = (bf16[2,128,2,8,128,1,1]{4,3,1,2,0,6,5:T(8,128)(2,1)}, bf16[2,128,2,8,128,1,1]{4,3,1,2,0,6,5:T(8,128)(2,1)S(1)}) fusion(bf16[1,1,256,2,8,128]{5,4,2,3,1,0:T(8,128)(2,1)S(1)} %get-tuple-element.30, bf16[1,1,256,2,8,128]{5,4,2,3,1,0:T(8,128)(2,1)} %get-tuple-element.31), kind=kLoop, calls=%fused_computation.20 | loop fusion | flops 1048576 | bytes 4194304 | tf_op jit(solution)/shard_map/reshape.11
  81.4 1.3 copy.42
  82.7 2.1 %copy.43 = bf16[1,32,2,3,512]{1,4,3,2,0:T(8,128)(2,1)} copy(bf16[1,32,2,3,512]{4,1,3,2,0:T(8,128)(2,1)} %collective-permute-done.8) | data formatting | bytes 393216 | tf_op jit(solution)/shard_map/ppermute | solution.py:17
  84.8 1.9 %maximum_bitcast_fusion.2 = bf16[128,2,3,512]{0,3,2,1:T(8,128)(2,1)S(1)} fusion(bf16[1,32,2,3,512]{1,4,3,2,0:T(8,128)(2,1)} %copy.43, bf16[1,64,2,3,512]{1,4,3,2,0:T(8,128)(2,1)S(1)} %dynamic_update_slice.34, bf16[1,32,2,3,512]{1,4,3,2,0:T(8,128)(2,1)S(1)} %copy.42), kind=kLoop, calls=%fused_computation.31 | loop fusion | flops 2359296 | bytes 1572864 | tf_op jit(solution)/shard_map/squeeze | solution.py:99
  86.8 1.5 fusion.44
  88.4 1.5 copy.71
  89.9 2.3 %copy.72 = bf16[128,2,3,4,128]{4,0,1,3,2:T(8,128)(2,1)} copy(bf16[128,2,3,4,128]{0,4,3,2,1:T(8,128)(2,1)} %get-tuple-element.24) | data formatting | bytes 1572864
  92.2 1.9 %fusion.29 = f32[2,8,128,128,3,4,1]{3,2,6,5,4,1,0:T(8,128)S(1)} fusion(bf16[2,128,2,8,128,1,1]{4,3,1,2,0,6,5:T(8,128)(2,1)S(1)} %get-tuple-element.14, bf16[128,2,3,4,128]{4,0,1,3,2:T(8,128)(2,1)S(1)} %copy.71), kind=kOutput, calls=%fused_computation.26 | convolution fusion | flops 1610612736 | bytes 14417920 | tf_op jit(solution)/shard_map/ipcbq,xpqsrj->ixsrcbj/dot_general | solution.py:45
  94.1 3.3 %fusion = bf16[2,8,128,128,3,4]{3,2,5,4,1,0:T(8,128)(2,1)S(1)} fusion(f32[2,8,128,128,3,4,1]{3,2,6,5,4,1,0:T(8,128)S(1)} %fusion.29, bf16[2,128,2,8,128,1,1]{4,3,1,2,0,6,5:T(8,128)(2,1)S(1)} %copy-done.1, bf16[128,2,3,4,128]{4,0,1,3,2:T(8,128)(2,1)} %copy.72), kind=kOutput, calls=%fused_computation.1 | convolution fusion | flops 1616904192 | bytes 20709376 | tf_op jit(solution)/shard_map/ipcbq,xpqsrj->ixsrcbj/dot_general | solution.py:48
  97.4 2.2 %fusion.21 = f32[64,512]{1,0:T(8,128)S(1)} fusion(bf16[128,2,8,3,512,1]{0,4,3,2,1,5:T(8,128)(2,1)S(1)} %bitcast.118, bf16[2,64,2,8,128,1]{4,3,1,2,0,5:T(8,128)(2,1)S(1)} %maximum_bitcast_fusion.3), kind=kOutput, calls=%fused_computation.16 | convolution fusion | flops 805666816 | bytes 6946816 | tf_op jit(solution)/shard_map/while/body/eval_jaxpr/xoiprk,kxprcw->xoicw/dot_general | solution.py:107
  99.6 0.7 broadcast_multiply_fusion
  100.3 64.4 %reduce-scatter.2.cloned.1.call-done = f32[8,512]{1,0:T(8,128)} async-done(((f32[64,512]{1,0:T(8,128)}), f32[8,512]{1,0:T(8,128)}) %reduce-scatter.2.cloned.1.call-update) | async-done | bytes 16400 | tf_op jit(solution)/shard_map/reduce_scatter | solution.py:115
  (22 shorter events, 0.4 us)
Async XLA Ops:
  6.5 6.9 %copy-start = (bf16[1,2,8,65]{3,2,1,0:T(8,128)(2,1)S(1)}, bf16[1,2,8,65]{3,2,1,0:T(8,128)(2,1)}, u32[]{:S(2)}) copy-start(bf16[1,2,8,65]{3,2,1,0:T(8,128)(2,1)} %param.5) | copy-start | bytes 6244
  6.5 158.2 %reduce-scatter.2.cloned.1.call-start = ((), (), s32[]{:S(2)}) async-start(), calls=%async_computation.1 | async-start | bytes 147456 | tf_op jit(solution)/shard_map/reduce_scatter | solution.py:115
  7.4 8.4 %collective-permute-start = (bf16[1,8,2,3,512]{4,1,3,2,0:T(8,128)(2,1)S(1)}, bf16[1,8,2,3,512]{4,1,3,2,0:T(8,128)(2,1)S(1)}, u32[]{:S(2)}, u32[]{:S(2)}) collective-permute-start(bf16[1,8,2,3,512]{4,1,3,2,0:T(8,128)(2,1)S(1)} %copy.31), channel_id=1, source_target_pairs={{0,2},{2,4},{4,6},{6,8},{8,10},{10,12},{12,14},{14,0},{1,3},{3,5},... | collective-permute-start | bytes 147464 | tf_op jit(solution)/shard_map/ppermute | solution.py:87
  10.3 6.2 %collective-permute-start.1 = (bf16[1,8,2,3,512]{4,1,3,2,0:T(8,128)(2,1)S(1)}, bf16[1,8,2,3,512]{4,1,3,2,0:T(8,128)(2,1)S(1)}, u32[]{:S(2)}, u32[]{:S(2)}) collective-permute-start(bf16[1,8,2,3,512]{4,1,3,2,0:T(8,128)(2,1)S(1)} %copy.31), channel_id=1, source_target_pairs={{0,14},{2,0},{4,2},{6,4},{8,6},{10,8},{12,10},{14,12},{1,15},{3,1}... | collective-permute-start | bytes 147464 | tf_op jit(solution)/shard_map/ppermute | solution.py:92
  14.6 0.7 copy-start.3
  15.8 14.8 %copy-start.2 = (bf16[1,8,2,3,512]{4,2,3,1,0:T(2,128)(2,1)S(1)}, bf16[1,8,2,3,512]{4,2,3,1,0:T(2,128)(2,1)}, u32[]{:S(2)}) copy-start(bf16[1,8,2,3,512]{4,2,3,1,0:T(2,128)(2,1)} %param.4) | copy-start | bytes 147460
  15.8 6.8 %collective-permute-start.2 = (bf16[1,8,2,3,512]{4,1,3,2,0:T(8,128)(2,1)S(1)}, bf16[1,8,2,3,512]{4,1,3,2,0:T(8,128)(2,1)S(1)}, u32[]{:S(2)}, u32[]{:S(2)}) collective-permute-start(bf16[1,8,2,3,512]{4,1,3,2,0:T(8,128)(2,1)S(1)} %collective-permute-done), channel_id=1, source_target_pairs={{0,2},{2,4},{4,6},{6,8},{8,10},{10,12},{12,14},{14,0},{1,3},{3,5},... | collective-permute-start | bytes 147464 | tf_op jit(solution)/shard_map/ppermute | solution.py:87
  16.6 6.5 %collective-permute-start.3 = (bf16[1,8,2,3,512]{4,1,3,2,0:T(8,128)(2,1)S(1)}, bf16[1,8,2,3,512]{4,1,3,2,0:T(8,128)(2,1)S(1)}, u32[]{:S(2)}, u32[]{:S(2)}) collective-permute-start(bf16[1,8,2,3,512]{4,1,3,2,0:T(8,128)(2,1)S(1)} %collective-permute-done.1), channel_id=1, source_target_pairs={{0,14},{2,0},{4,2},{6,4},{8,6},{10,8},{12,10},{14,12},{1,15},{3,1}... | collective-permute-start | bytes 147464 | tf_op jit(solution)/shard_map/ppermute | solution.py:92
  22.6 6.8 %collective-permute-start.4 = (bf16[1,8,2,3,512]{4,1,3,2,0:T(8,128)(2,1)S(1)}, bf16[1,8,2,3,512]{4,1,3,2,0:T(8,128)(2,1)S(1)}, u32[]{:S(2)}, u32[]{:S(2)}) collective-permute-start(bf16[1,8,2,3,512]{4,1,3,2,0:T(8,128)(2,1)S(1)} %collective-permute-done.2), channel_id=1, source_target_pairs={{0,2},{2,4},{4,6},{6,8},{8,10},{10,12},{12,14},{14,0},{1,3},{3,5},... | collective-permute-start | bytes 147464 | tf_op jit(solution)/shard_map/ppermute | solution.py:87
  23.0 37.8 %collective-permute-start.5 = (bf16[1,8,2,3,512]{4,1,3,2,0:T(8,128)(2,1)S(1)}, bf16[1,8,2,3,512]{4,1,3,2,0:T(8,128)(2,1)S(1)}, u32[]{:S(2)}, u32[]{:S(2)}) collective-permute-start(bf16[1,8,2,3,512]{4,1,3,2,0:T(8,128)(2,1)S(1)} %collective-permute-done.3), channel_id=1, source_target_pairs={{0,14},{2,0},{4,2},{6,4},{8,6},{10,8},{12,10},{14,12},{1,15},{3,1}... | collective-permute-start | bytes 147464 | tf_op jit(solution)/shard_map/ppermute | solution.py:92
  29.4 36.8 %collective-permute-start.6 = (bf16[1,8,2,3,512]{4,1,3,2,0:T(8,128)(2,1)S(1)}, bf16[1,8,2,3,512]{4,1,3,2,0:T(8,128)(2,1)S(1)}, u32[]{:S(2)}, u32[]{:S(2)}) collective-permute-start(bf16[1,8,2,3,512]{4,1,3,2,0:T(8,128)(2,1)S(1)} %collective-permute-done.4), channel_id=1, source_target_pairs={{0,2},{2,4},{4,6},{6,8},{8,10},{10,12},{12,14},{14,0},{1,3},{3,5},... | collective-permute-start | bytes 147464 | tf_op jit(solution)/shard_map/ppermute | solution.py:87
  72.9 8.5 %collective-permute-start.7 = (bf16[1,32,2,3,512]{4,1,3,2,0:T(8,128)(2,1)}, bf16[1,32,2,3,512]{4,1,3,2,0:T(8,128)(2,1)}, u32[]{:S(2)}, u32[]{:S(2)}) collective-permute-start(bf16[1,32,2,3,512]{4,1,3,2,0:T(8,128)(2,1)} %copy.40), channel_id=1, source_target_pairs={{0,1},{2,3},{4,5},{6,7},{8,9},{10,11},{12,13},{14,15},{16,17},{18,... | collective-permute-start | bytes 589832 | tf_op jit(solution)/shard_map/ppermute | solution.py:15
  75.8 6.9 %collective-permute-start.8 = (bf16[1,32,2,3,512]{4,1,3,2,0:T(8,128)(2,1)}, bf16[1,32,2,3,512]{4,1,3,2,0:T(8,128)(2,1)}, u32[]{:S(2)}, u32[]{:S(2)}) collective-permute-start(bf16[1,32,2,3,512]{4,1,3,2,0:T(8,128)(2,1)} %copy.41), channel_id=1, source_target_pairs={{1,0},{3,2},{5,4},{7,6},{9,8},{11,10},{13,12},{15,14},{17,16},{19,... | collective-permute-start | bytes 589832 | tf_op jit(solution)/shard_map/ppermute | solution.py:17
  92.2 1.9 %copy-start.1 = (bf16[2,128,2,8,128,1,1]{4,3,1,2,0,6,5:T(8,128)(2,1)S(1)}, bf16[2,128,2,8,128,1,1]{4,3,1,2,0,6,5:T(8,128)(2,1)}, u32[]{:S(2)}) copy-start(bf16[2,128,2,8,128,1,1]{4,3,1,2,0,6,5:T(8,128)(2,1)} %get-tuple-element.13) | copy-start | bytes 3145732
Sparse Core Ops, SparseCore 0:
  100.4 64.2 reduce-scatter.1
